TPU v7x, 256 devices: a whole 4x4x8 slice. The times are simulated.
256 devices in a mesh: chan: 16 (over x, y), tm: 16 (over z, core).
Axes of the slice: x: 4, y: 4, z: 8, core: 2. Of those that a mesh axis runs over, the one named last changes fastest.
Arguments:
- records: bfloat16 [16, 6144, 1536], P('tm', 'chan')
- partners: int32 [16, 3], P('chan'), may hold values from 0 to 15, as said below
- counts: int32 [16], P('chan'), may hold values from 1 to 3, as said below
- sources: int32 [16, 2], P('chan'), may hold values from 0 to 383, as said below
Outputs:
- xcorr: float32 [16, 384, 3, 2, 384], P('chan', 'tm')
Inputs may be any that keep to these rules, and one draw needn't show every extreme that they name: `partners`: each row holds 3 different blocks. `counts`: some block has all 3 slots live. `sources`: each row holds 2 different channels.
All inputs are finite; a program needn't handle non-finite values.
Results may differ from a plain program's by a relative error of at most 0.008.
Values may be sent and summed in bfloat16 or wider, within the bound.
A program may use at most 64 MiB of HBM per device.

v0:
```python
import math
import jax
import jax.numpy as jnp
from jax import lax
from jax.sharding import PartitionSpec as P

L = 1536
F = 320
HL = 192
SMOOTH = 32


def dft_table(length, bins):
    sample_index = jnp.arange(length, dtype=jnp.int32)[:, None]
    bin_index = jnp.arange(bins, dtype=jnp.int32)[None, :] + 1
    phase_index = sample_index * bin_index % length
    angle = phase_index.astype(jnp.float32) * (2.0 * math.pi / length)
    return jnp.concatenate([jnp.cos(angle), -jnp.sin(angle)], axis=1).astype(jnp.bfloat16)


def lag_table(length, bins, half):
    bin_index = jnp.arange(bins, dtype=jnp.int32)[:, None] + 1
    lag_index = jnp.arange(2 * half, dtype=jnp.int32)[None, :] - half
    phase_index = jnp.mod(bin_index * lag_index, length)
    angle = phase_index.astype(jnp.float32) * (2.0 * math.pi / length)
    return jnp.concatenate([jnp.cos(angle), -jnp.sin(angle)], axis=0)


def band_table(bins, half):
    input_bin = jnp.arange(bins, dtype=jnp.int32)[:, None]
    output_bin = jnp.arange(bins, dtype=jnp.int32)[None, :]
    centre = jnp.clip(output_bin, half, bins - 1 - half)
    return (jnp.abs(input_bin - centre) <= half).astype(jnp.float32)


def whiten(block_records):
    windows, channels, length = block_records.shape
    signal = block_records.astype(jnp.float32)
    signal = signal - jnp.mean(signal, axis=-1, keepdims=True)
    demeaned = signal.astype(jnp.bfloat16).reshape(windows * channels, length)
    spectrum = jnp.dot(demeaned, dft_table(L, F), preferred_element_type=jnp.float32)
    real_part = spectrum[:, :F]
    imag_part = spectrum[:, F:]
    amplitude = jnp.sqrt(real_part * real_part + imag_part * imag_part)
    smooth = jnp.dot(amplitude, band_table(F, SMOOTH), precision=lax.Precision.HIGHEST) / (
        2 * SMOOTH + 1
    )
    factor = 1.0 / (smooth + 1e-06)
    whitened = jnp.concatenate([real_part * factor, imag_part * factor], axis=1)
    return whitened.astype(jnp.bfloat16).reshape(windows, channels, 2 * F)


def cross_terms(source_spec, partner_white):
    src_real = source_spec[..., :F]
    src_imag = source_spec[..., F:]
    rec_real = partner_white[..., :F]
    rec_imag = partner_white[..., F:]
    cross_real = jnp.einsum(
        "wsf,pwcf->cpsf", src_real, rec_real, preferred_element_type=jnp.float32
    ) + jnp.einsum("wsf,pwcf->cpsf", src_imag, rec_imag, preferred_element_type=jnp.float32)
    cross_imag = jnp.einsum(
        "wsf,pwcf->cpsf", src_real, rec_imag, preferred_element_type=jnp.float32
    ) - jnp.einsum("wsf,pwcf->cpsf", src_imag, rec_real, preferred_element_type=jnp.float32)
    return jnp.concatenate([cross_real, cross_imag], axis=-1)


def local(records, partners, counts, sources):
    windows, channels, length = records.shape
    slots = partners.shape[1]
    white = whiten(records)
    partner_ids = partners[0]
    live = jnp.arange(slots, dtype=jnp.int32) < counts[0]
    piece = lax.all_gather(white, "chan", axis=1, tiled=True)
    blocks_here = piece.shape[1] // channels
    block_ids = jnp.arange(blocks_here, dtype=jnp.int32)
    matches = ((block_ids[None, :] == partner_ids[:, None]) & live[:, None]).astype(jnp.bfloat16)
    shaped = piece.reshape(windows, blocks_here, channels, piece.shape[2])
    partner_white = jnp.einsum(
        "pj,wjcf->pwcf", matches, shaped, preferred_element_type=jnp.float32
    ).astype(jnp.bfloat16)
    picker = (jnp.arange(channels, dtype=jnp.int32)[None, :] == sources[0][:, None]).astype(
        jnp.bfloat16
    )
    source_spec = jnp.einsum(
        "sc,wcf->wsf", picker, white, preferred_element_type=jnp.float32
    ).astype(jnp.bfloat16)
    sources_count = source_spec.shape[1]
    inverse = lag_table(L, F, HL)
    scale = 1.0 / math.sqrt(F * windows * lax.axis_size("tm"))
    share_rows = channels // lax.axis_size("tm")
    stacked = cross_terms(source_spec, partner_white)
    summed = lax.psum_scatter(stacked, "tm", scatter_dimension=0, tiled=True)
    lagged = jnp.dot(
        summed.reshape(share_rows * slots * sources_count, 2 * F),
        inverse,
        precision=lax.Precision.HIGHEST,
    )
    result = lagged.reshape(share_rows, slots, sources_count, 2 * HL) * scale
    return result[None]


def solution(mesh):
    return jax.shard_map(
        local,
        mesh=mesh,
        in_specs=(P("tm", "chan", None), P("chan", None), P("chan"), P("chan", None)),
        out_specs=P("chan", "tm", None, None, None),
        check_vma=False,
    )
```

profile of v0, /device:TPU:2, one launch (start us, length us, event | category | flops | bytes accessed | tf_op | source)
XLA Modules:
  0.0 186.4 jit_solution(6916343911090276861)
XLA Ops:
  6.5 0.0 copy-start
  6.5 0.0 all-gather.2.cloned.1.call-start
  6.5 10.0 %cosine_convert_fusion = (bf16[1536,320]{1,0:T(8,128)(2,1)S(1)}, bf16[1536,320]{1,0:T(8,128)(2,1)S(1)}) fusion(s32[320]{0:T(512)S(1)} %iota_add_fusion.1), kind=kLoop, calls=%fused_computation.14 | loop fusion | flops 5898240 | bytes 1967360 | tf_op jit(solution)/shard_map/convert.30
  16.6 0.0 copy-done
  16.6 0.2 convert_reduce_fusion
  16.8 1.2 fusion.8
  18.0 0.0 copy-start.2
  18.0 0.0 copy-start.1
  18.0 1.1 multiply_convert_fusion.1
  19.1 1.0 pad_maximum_fusion.1
  20.0 0.0 all-gather.2.cloned.1.call-update
  20.1 0.2 reduce-scatter.2.cloned.1.call-start
  21.0 0.0 copy-done.2
  21.0 0.3 fusion.20
  21.2 0.1 convert_bitcast_fusion.4
  21.3 75.4 %all-gather.2.cloned.1.call-done = bf16[1,6144,640]{2,1,0:T(8,128)(2,1)} async-done(((bf16[1,384,640]{2,1,0:T(8,128)(2,1)}), bf16[1,6144,640]{2,1,0:T(8,128)(2,1)}) %all-gather.2.cloned.1.call-update) | async-done | bytes 7864336 | tf_op jit(solution)/shard_map/all_gather | solution.py:73
  96.7 0.0 copy-done.1
  96.7 7.9 %convert_bitcast_fusion.2 = bf16[3,1,384,640]{3,0,2,1:T(4,128)(2,1)S(1)} fusion(bf16[16,384,640]{2,1,0:T(8,128)(2,1)} %bitcast.59, s32[3]{0:T(128)S(1)} %bitcast.62, pred[3]{0:T(512)(128)(4,1)S(1)} %iota_compare_fusion.1), kind=kOutput, calls=%fused_computation.23 | convolution fusion | flops 24330336 | bytes 9338895 | tf_op jit(solution)/shard_map/pj,wjcf->pwcf/dot_general | solution.py:78
  104.6 1.2 convert_bitcast_fusion.1
  105.8 0.1 copy.7
  105.9 0.1 copy.8
  106.0 0.9 add_bitcast_fusion
  106.9 3.6 %pad_maximum_fusion = f32[384,3,2,640]{3,0,2,1:T(8,128)} fusion(f32[384,3,2,320]{3,0,2,1:T(8,128)S(1)} %get-tuple-element.6, f32[384,3,2,320]{3,0,2,1:T(8,128)S(1)} %get-tuple-element.5), kind=kLoop, calls=%fused_computation.2 | loop fusion | flops 1474560 | bytes 11796480 | tf_op jit(solution)/shard_map/concatenate | solution.py:64
  110.5 0.0 reduce-scatter.2.cloned.1.call-update
  110.6 2.1 %fusion.36 = (f32[320,384]{1,0:T(8,128)S(1)}, f32[320,384]{1,0:T(8,128)S(1)}) fusion(s32[384]{0:T(512)S(1)} %iota_add_fusion, s32[320]{0:T(512)S(1)} %iota_add_fusion.1), kind=kLoop, calls=%fused_computation.57 | loop fusion | flops 1228800 | bytes 985856 | tf_op jit(solution)/shard_map/cos | solution.py:26
  112.6 64.2 %reduce-scatter.2.cloned.1.call-done = f32[24,3,2,640]{3,0,2,1:T(8,128)} async-done(((f32[384,3,2,640]{3,0,2,1:T(8,128)}), f32[24,3,2,640]{3,0,2,1:T(8,128)}) %reduce-scatter.2.cloned.1.call-update) | async-done | bytes 368656 | tf_op jit(solution)/shard_map/reduce_scatter | solution.py:92
  176.8 1.9 %fusion.19 = f32[1,24,3,2,384]{4,1,3,2,0:T(8,128)S(1)} fusion(f32[24,3,2,640]{3,0,2,1:T(8,128)} %reduce-scatter.2.cloned.1.call-done, f32[320,384]{1,0:T(8,128)S(1)} %get-tuple-element.12, f32[320,384]{1,0:T(8,128)S(1)} %get-tuple-element.11), kind=kOutput, calls=%fused_computation.32 | convolution fusion | flops 424974336 | bytes 1572864 | tf_op jit(solution)/shard_map/dot_general | solution.py:93
  178.7 0.8 copy.9
  (5 shorter events, 0.0 us)
Async XLA Ops:
  6.5 10.0 %copy-start = (bf16[1,384,1536]{2,1,0:T(8,128)(2,1)S(1)}, bf16[1,384,1536]{2,1,0:T(8,128)(2,1)}, u32[]{:S(2)}) copy-start(bf16[1,384,1536]{2,1,0:T(8,128)(2,1)} %param.4) | copy-start | bytes 3538948
  6.5 90.1 %all-gather.2.cloned.1.call-start = ((), (), s32[]{:S(2)}) async-start(), calls=%async_computation.1 | async-start | bytes 8355840 | tf_op jit(solution)/shard_map/all_gather | solution.py:73
  18.0 3.0 %copy-start.2 = (s32[1,2]{1,0:T(1,128)S(1)}, s32[1,2]{1,0:T(1,128)}, u32[]{:S(2)}) copy-start(s32[1,2]{1,0:T(1,128)} %param.7) | copy-start | bytes 28
  18.0 78.7 %copy-start.1 = (s32[1,3]{1,0:T(1,128)S(1)}, s32[1,3]{1,0:T(1,128)}, u32[]{:S(2)}) copy-start(s32[1,3]{1,0:T(1,128)} %param.5) | copy-start | bytes 40
  20.1 156.7 %reduce-scatter.2.cloned.1.call-start = ((), (), s32[]{:S(2)}) async-start(), calls=%async_computation.2 | async-start | bytes 6266880 | tf_op jit(solution)/shard_map/reduce_scatter | solution.py:92
Sparse Core Ops, SparseCore 0:
  20.2 76.4 all-gather.1
  110.7 66.0 reduce-scatter.1
where the time goes:
time: 187 us; the launch traced here: 186 us
  waiting for transfers between devices  140 us (75%)
  other arithmetic  19.1 us (10%)
  between operations  14.2 us (8%)
  matrix products  12.3 us (7%)
    all_gather x1, waiting for transfers between devices, local(): piece = lax.all_gather(white, 'chan', axis=1, tiled=True)  75.4 us
    reduce_scatter x1, waiting for transfers between devices, local(): summed = lax.psum_scatter(stacked, 'tm', scatter_dimension=0, tiled=True)  64.2 us
    another operation x3, other arithmetic  11.2 us
    dot_general x1, matrix products, local(): jnp.einsum('pj,wjcf->pwcf', matches, shaped, preferred_element_type=jnp.f...  7.9 us
  transfers between devices with their start and end apart: 2, of which 2 were waited for; matrix products, arithmetic and copies ran while one was open for 1% of the time, Pallas kernels for 0%

commit v1 on v0

--- a/solution.py
+++ b/solution.py
@@ -1,3 +1,4 @@
+import functools
 import math
 import jax
 import jax.numpy as jnp
@@ -8,6 +9,19 @@
 F = 320
 HL = 192
 SMOOTH = 32
+
+
+def sheet_map(block_in, axis_key):
+    response = jax.lax.all_to_all(
+        jnp.stack(jax.lax.axis_size(axis_key) * [block_in], axis=0),
+        axis_name=axis_key,
+        split_axis=0,
+        concat_axis=0,
+    )
+    return jnp.concatenate(response, 1)
+
+
+record_meet = functools.partial(sheet_map, axis_key="chan")
 
 
 def dft_table(length, bins):
@@ -70,7 +84,7 @@
     white = whiten(records)
     partner_ids = partners[0]
     live = jnp.arange(slots, dtype=jnp.int32) < counts[0]
-    piece = lax.all_gather(white, "chan", axis=1, tiled=True)
+    piece = record_meet(white)
     blocks_here = piece.shape[1] // channels
     block_ids = jnp.arange(blocks_here, dtype=jnp.int32)
     matches = ((block_ids[None, :] == partner_ids[:, None]) & live[:, None]).astype(jnp.bfloat16)

time: 187 us -> 263 us (1.41)
  waiting for transfers between devices: 140 us -> 205 us
  starting transfers between devices: 0.22 us -> 7.83 us
  local copies, waits for them, and re-layouts: 1.05 us -> 5.11 us
    all_to_all x0 -> x1, waiting for transfers between devices: none -> 97.3 us  [sheet_map(): jax.lax.all_to_all(jnp.stack(jax.lax.axis_size(axis_key) * [block_in], ax...]
    all_gather x1 -> x0, waiting for transfers between devices: 75.4 us -> none  [local(): piece = lax.all_gather(white, 'chan', axis=1, tiled=True)]
    reduce_scatter x1, waiting for transfers between devices: 64.2 us -> 108 us  [local(): summed = lax.psum_scatter(stacked, 'tm', scatter_dimension=0, tiled=True)]
    all_to_all x0 -> x1, starting transfers between devices: none -> 7.61 us  [sheet_map(): jax.lax.all_to_all(jnp.stack(jax.lax.axis_size(axis_key) * [block_in], ax...]
    another operation x2 -> x3, local copies, waits for them, and re-layouts: 0.23 us -> 4.3 us  [the longest x1 4.07 us: sheet_map(): jnp.stack(jax.lax.axis_size(axis_key) * [block_in], axis=0)]
where the time goes in v1:
time: 263 us
  waiting for transfers between devices  205 us (78%)
  other arithmetic  18.2 us (7%)
  between operations  14.1 us (5%)
  matrix products  12.2 us (5%)
  starting transfers between devices  7.83 us (3%)
  local copies, waits for them, and re-layouts  5.11 us (2%)
    reduce_scatter x1, waiting for transfers between devices, local(): summed = lax.psum_scatter(stacked, 'tm', scatter_dimension=0, tiled=True)  108 us
    all_to_all x1, waiting for transfers between devices, sheet_map(): jax.lax.all_to_all(jnp.stack(jax.lax.axis_size(axis_key) * [block_in], ax...  97.3 us
    another operation x3, other arithmetic  11.2 us
    dot_general x1, matrix products, local(): jnp.einsum('pj,wjcf->pwcf', matches, shaped, preferred_element_type=jnp.f...  7.9 us
    all_to_all x1, starting transfers between devices, sheet_map(): jax.lax.all_to_all(jnp.stack(jax.lax.axis_size(axis_key) * [block_in], ax...  7.61 us
  transfers between devices with their start and end apart: 2, of which 2 were waited for; matrix products, arithmetic and copies ran while one was open for 1% of the time, Pallas kernels for 0%

profile of v1, /device:TPU:2, one launch (start us, length us, event | category | flops | bytes accessed | tf_op | source)
XLA Modules:
  0.0 262.8 jit_solution(18332548738708405152)
XLA Ops:
  6.5 0.0 copy-start
  6.5 10.0 %cosine_convert_fusion = (bf16[1536,320]{1,0:T(8,128)(2,1)S(1)}, bf16[1536,320]{1,0:T(8,128)(2,1)S(1)}) fusion(s32[320]{0:T(512)S(1)} %iota_add_fusion.1), kind=kLoop, calls=%fused_computation.15 | loop fusion | flops 5898240 | bytes 1967360 | tf_op jit(solution)/shard_map/convert.26
  16.5 0.0 copy-done
  16.6 0.2 convert_reduce_fusion
  16.8 1.2 fusion.9
  18.0 1.1 multiply_convert_fusion.1
  19.0 0.2 pad_maximum_fusion.1
  19.2 4.1 %stack.3 = bf16[16,1,384,640]{3,2,1,0:T(8,128)(2,1)} broadcast(bf16[384,640]{1,0:T(8,128)(2,1)S(1)} %pad_maximum_fusion.1), dimensions={2,3} | broadcast | bytes 8355840 | tf_op jit(solution)/shard_map/stack | solution.py:16
  23.3 0.0 copy-start.2
  23.3 0.0 copy-start.1
  23.3 7.6 %all-to-all-start = ((bf16[16,1,384,640]{3,2,1,0:T(8,128)(2,1)}), bf16[16,1,384,640]{3,2,1,0:T(8,128)(2,1)}, u32[]{:S(2)}, u32[]{:S(2)}) async-start(bf16[16,1,384,640]{3,2,1,0:T(8,128)(2,1)} %stack.3), calls=%async_computation | async-start | bytes 15728640 | tf_op jit(solution)/shard_map/all_to_all | solution.py:15
  30.9 0.2 reduce-scatter.2.cloned.1.call-start
  31.8 0.0 copy-done.2
  31.8 0.2 fusion.21
  32.0 0.1 convert_bitcast_fusion.4
  32.1 97.3 %all-to-all-done = bf16[16,1,384,640]{3,2,1,0:T(8,128)(2,1)} async-done(((bf16[16,1,384,640]{3,2,1,0:T(8,128)(2,1)}), bf16[16,1,384,640]{3,2,1,0:T(8,128)(2,1)}, u32[]{:S(2)}, u32[]{:S(2)}) %all-to-all-start) | async-done | bytes 7864352 | tf_op jit(solution)/shard_map/all_to_all | solution.py:15
  129.4 0.0 copy-done.1
  129.4 7.9 %convert_bitcast_fusion.2 = bf16[3,1,384,640]{3,0,2,1:T(4,128)(2,1)S(1)} fusion(bf16[16,1,384,640]{3,2,1,0:T(8,128)(2,1)} %all-to-all-done, s32[3]{0:T(128)S(1)} %bitcast.62, pred[3]{0:T(512)(128)(4,1)S(1)} %iota_compare_fusion.1), kind=kOutput, calls=%fused_computation.24 | convolution fusion | flops 24330336 | bytes 9338895 | tf_op jit(solution)/shard_map/pj,wjcf->pwcf/dot_general | solution.py:92
  137.3 1.2 convert_bitcast_fusion.1
  138.4 0.1 copy.12
  138.6 0.1 copy.11
  138.7 0.9 add_bitcast_fusion
  139.6 3.6 %pad_maximum_fusion = f32[384,3,2,640]{3,0,2,1:T(8,128)} fusion(f32[384,3,2,320]{3,0,2,1:T(8,128)S(1)} %get-tuple-element.6, f32[384,3,2,320]{3,0,2,1:T(8,128)S(1)} %get-tuple-element.5), kind=kLoop, calls=%fused_computation.3 | loop fusion | flops 1474560 | bytes 11796480 | tf_op jit(solution)/shard_map/concatenate | solution.py:78
  143.2 0.0 reduce-scatter.2.cloned.1.call-update
  143.2 2.1 fusion.34
  145.3 107.9 %reduce-scatter.2.cloned.1.call-done = f32[24,3,2,640]{3,0,2,1:T(8,128)} async-done(((f32[384,3,2,640]{3,0,2,1:T(8,128)}), f32[24,3,2,640]{3,0,2,1:T(8,128)}) %reduce-scatter.2.cloned.1.call-update) | async-done | bytes 368656 | tf_op jit(solution)/shard_map/reduce_scatter | solution.py:106
  253.2 1.9 fusion.20
  255.1 0.8 copy.13
  (5 shorter events, 0.0 us)
Async XLA Ops:
  6.5 10.0 %copy-start = (bf16[1,384,1536]{2,1,0:T(8,128)(2,1)S(1)}, bf16[1,384,1536]{2,1,0:T(8,128)(2,1)}, u32[]{:S(2)}) copy-start(bf16[1,384,1536]{2,1,0:T(8,128)(2,1)} %param.4) | copy-start | bytes 3538948
  23.3 8.5 %copy-start.2 = (s32[1,2]{1,0:T(1,128)S(1)}, s32[1,2]{1,0:T(1,128)}, u32[]{:S(2)}) copy-start(s32[1,2]{1,0:T(1,128)} %param.7) | copy-start | bytes 28
  23.3 106.1 %copy-start.1 = (s32[1,3]{1,0:T(1,128)S(1)}, s32[1,3]{1,0:T(1,128)}, u32[]{:S(2)}) copy-start(s32[1,3]{1,0:T(1,128)} %param.5) | copy-start | bytes 40
  23.3 106.1 %all-to-all-start = ((bf16[16,1,384,640]{3,2,1,0:T(8,128)(2,1)}), bf16[16,1,384,640]{3,2,1,0:T(8,128)(2,1)}, u32[]{:S(2)}, u32[]{:S(2)}) async-start(bf16[16,1,384,640]{3,2,1,0:T(8,128)(2,1)} %stack.3), calls=%async_computation | async-start | bytes 15728640 | tf_op jit(solution)/shard_map/all_to_all | solution.py:15
  30.9 222.4 %reduce-scatter.2.cloned.1.call-start = ((), (), s32[]{:S(2)}) async-start(), calls=%async_computation.2 | async-start | bytes 6266880 | tf_op jit(solution)/shard_map/reduce_scatter | solution.py:106
Sparse Core Ops, SparseCore 0:
  143.3 109.8 reduce-scatter.1
